TPU v7x, 512 devices: a whole 4x4x16 slice. The times are simulated.
512 devices in a mesh: band: 128 (over z, y, x_lo), domain: 4 (over x_hi, core).
Axes of the slice: x: 4 (x_hi: 2, x_lo: 2; x = x_hi * 2 + x_lo), y: 4, z: 16, core: 2. Of those that a mesh axis runs over, the one named last changes fastest.
Arguments:
- orbitals: bfloat16 [1024, 8, 5120], P('band', 'domain'), may hold values from -6 to 6
- boundary: bfloat16 [1024, 4, 5120], P('band'), may hold values from -6 to 6
- potential: bfloat16 [8, 5120], P('domain'), may hold values from 0 to 2
Outputs:
- correlation: float32 [1024, 1024], P('band', 'domain')
- projected: float32 [1024, 1024], P('band', 'domain')
All inputs are finite; a program needn't handle non-finite values.
Results may differ from a plain program's by a relative error of at most 0.0012.
Values may be sent and summed in bfloat16 or wider, within the bound.
No kernel may reach another device: no remote copies, remote signals or barrier semaphores. Data moves between devices by JAX's collectives and lax.ppermute only.
A program may use at most 128 MiB of HBM per device.

v0:
```python
import jax
import jax.numpy as jnp
from jax import lax
from jax.sharding import PartitionSpec as P

NX = 160
NY = 32
NZ_DEV = 2
DEGREE = 4
filter_center = 5.5
filter_radius = 4.5


def padded_2(cells, sides, width):
    for axis, dim in sides:
        count = lax.axis_size(axis)
        ends = count - 1
        head = lax.slice_in_dim(cells, 0, width, axis=dim)
        tail = lax.slice_in_dim(cells, cells.shape[dim] - width, cells.shape[dim], axis=dim)
        cells = jnp.concatenate(
            [
                lax.ppermute(tail, axis, [(i, (i + 1) % count) for i in range(ends)]),
                cells,
                lax.ppermute(head, axis, [((i + 1) % count, i) for i in range(ends)]),
            ],
            axis=dim,
        )
    return cells


def second_diff(values, axis_pos):
    near = jnp.roll(values, 1, axis_pos) + jnp.roll(values, -1, axis_pos)
    far = jnp.roll(values, 2, axis_pos) + jnp.roll(values, -2, axis_pos)
    return (16.0 * near - far - 30.0 * values) / 12.0


def plane_part(values):
    shaped = values.reshape(values.shape[:-1] + (NY, NX))
    total = second_diff(shaped, -1) + second_diff(shaped, -2)
    return total.reshape(values.shape)


def hamiltonian(padded, potential):
    middle = padded[:, 2:-2]
    z_part = (
        16.0 * (padded[:, 1:-3] + padded[:, 3:-1])
        - (padded[:, :-4] + padded[:, 4:])
        - 30.0 * middle
    ) / 12.0
    laplace = z_part + plane_part(middle)
    return -0.5 * laplace + potential.astype(jnp.float32) * middle


def chebyshev(apply_ham, orb_block):
    earlier = orb_block
    current = (
        (apply_ham(orb_block) - filter_center * orb_block.astype(jnp.float32)) / filter_radius
    ).astype(jnp.bfloat16)
    for degree_step in range(DEGREE - 1):
        following = (
            2.0 * (apply_ham(current) - filter_center * current.astype(jnp.float32)) / filter_radius
        )
        following = (following - earlier.astype(jnp.float32)).astype(jnp.bfloat16)
        earlier, current = (current, following)
    return (current, apply_ham(current).astype(jnp.bfloat16))


def per_device(orbitals, boundary, potential):
    orb_count = orbitals.shape[0]
    domain_pos = lax.axis_index("domain")
    domain_count = lax.axis_size("domain")
    last_pos = domain_count - 1

    def apply_ham(values):
        padded = padded_2(values, (("domain", 1),), 2)
        lower_rim = jnp.where(domain_pos == 0, boundary[:, 0:2], padded[:, 0:2])
        upper_rim = jnp.where(domain_pos == last_pos, boundary[:, 2:4], padded[:, -2:])
        padded = jnp.concatenate([lower_rim, padded[:, 2:-2], upper_rim], axis=1).astype(
            jnp.float32
        )
        return hamiltonian(padded, potential)

    filtered, applied = chebyshev(apply_ham, orbitals)
    filtered = filtered.reshape(orb_count, -1)
    applied = applied.reshape(orb_count, -1)
    cell_y, cell_h = (
        lax.all_to_all(filtered, "band", split_axis=1, concat_axis=0, tiled=True),
        lax.all_to_all(applied, "band", split_axis=1, concat_axis=0, tiled=True),
    )
    cell_y, cell_h = (
        lax.all_gather(cell_y, "domain", axis=1, tiled=True),
        lax.all_gather(cell_h, "domain", axis=1, tiled=True),
    )
    column_count = cell_y.shape[0] // domain_count
    column_y = lax.dynamic_slice_in_dim(cell_y, domain_pos * column_count, column_count, 0)
    column_h = lax.dynamic_slice_in_dim(cell_h, domain_pos * column_count, column_count, 0)
    contract_dims = (((1,), (1,)), ((), ()))
    with_y = lax.dot_general(cell_y, column_y, contract_dims, preferred_element_type=jnp.float32)
    with_h = lax.dot_general(cell_y, column_h, contract_dims, preferred_element_type=jnp.float32)
    summed = lax.psum_scatter(
        jnp.concatenate([with_y, with_h], axis=1), "band", scatter_dimension=0, tiled=True
    )
    total_cells = NZ_DEV * NY * NX * domain_count
    correlation = summed[:, :column_count] / total_cells
    projected = summed[:, column_count:] / total_cells
    return (correlation, projected)


def solution(mesh):
    return jax.shard_map(
        per_device,
        mesh=mesh,
        in_specs=(P("band", "domain", None), P("band", None, None), P("domain", None)),
        out_specs=(P("band", "domain"), P("band", "domain")),
        check_vma=False,
    )
```

profile of v0, /device:TPU:4, one launch (start us, length us, event | category | flops | bytes accessed | tf_op | source)
XLA Modules:
  0.0 797.5 jit_solution(4684403561107533573)
XLA Ops:
  8.1 1.9 collective-permute-start.1
  10.0 2.4 collective-permute-start
  14.7 6.3 collective-permute-done
  29.2 1.9 collective-permute-start.3
  31.1 2.4 collective-permute-start.2
  34.0 5.3 collective-permute-done.2
  44.4 2.0 fusion.5
  47.9 1.9 collective-permute-start.5
  49.9 2.4 collective-permute-start.4
  52.7 5.3 collective-permute-done.4
  63.2 2.0 fusion.9
  66.6 1.9 collective-permute-start.7
  68.5 2.6 collective-permute-start.6
  71.4 5.3 collective-permute-done.6
  81.8 2.0 fusion.13
  85.3 1.9 collective-permute-start.9
  87.4 2.4 collective-permute-start.8
  91.0 19.2 %all-to-all-start = ((bf16[8,128,80]{2,0,1:T(8,128)(2,1)}), bf16[8,128,80]{2,0,1:T(8,128)(2,1)}, u32[]{:S(2)}, u32[]{:S(2)}) async-start(bf16[8,128,80]{2,0,1:T(8,128)(2,1)} %copy.26), calls=%async_computation | async-start | bytes 524288 | tf_op jit(solution)/shard_map/all_to_all | solution.py:87
  118.1 11.0 %all-to-all-done = bf16[8,128,80]{2,0,1:T(8,128)(2,1)} async-done(((bf16[8,128,80]{2,0,1:T(8,128)(2,1)}), bf16[8,128,80]{2,0,1:T(8,128)(2,1)}, u32[]{:S(2)}, u32[]{:S(2)}) %all-to-all-start) | async-done | bytes 163872 | tf_op jit(solution)/shard_map/all_to_all | solution.py:87
  129.1 9.1 %all-to-all-start.1 = ((bf16[8,128,80]{2,0,1:T(8,128)(2,1)}), bf16[8,128,80]{2,0,1:T(8,128)(2,1)S(1)}, u32[]{:S(2)}, u32[]{:S(2)}) async-start(bf16[8,128,80]{2,0,1:T(8,128)(2,1)} %copy.29), calls=%async_computation.1 | async-start | bytes 524288 | tf_op jit(solution)/shard_map/all_to_all | solution.py:88
  139.3 9.0 %all_gather.6 = bf16[1024,320]{0,1:T(8,128)(2,1)S(1)} all-gather(bf16[1024,80]{0,1:T(8,128)(2,1)S(1)} %copy.27), channel_id=1, replica_groups=mesh['band'=128,'domain'=4] {'domain'}, dimensions={1}, use_global_device_ids=true | all-gather | bytes 819200 | tf_op jit(solution)/shard_map/all_gather | solution.py:91
  148.9 8.1 %all-to-all-done.1 = bf16[8,128,80]{2,0,1:T(8,128)(2,1)S(1)} async-done(((bf16[8,128,80]{2,0,1:T(8,128)(2,1)}), bf16[8,128,80]{2,0,1:T(8,128)(2,1)S(1)}, u32[]{:S(2)}, u32[]{:S(2)}) %all-to-all-start.1) | async-done | bytes 163872 | tf_op jit(solution)/shard_map/all_to_all | solution.py:88
  157.1 8.4 %all_gather.7 = bf16[1024,320]{0,1:T(8,128)(2,1)S(1)} all-gather(bf16[1024,80]{0,1:T(8,128)(2,1)S(1)} %copy.30), channel_id=1, replica_groups=mesh['band'=128,'domain'=4] {'domain'}, dimensions={1}, use_global_device_ids=true | all-gather | bytes 819200 | tf_op jit(solution)/shard_map/all_gather | solution.py:92
  168.0 620.3 %reduce-scatter.4.cloned.1.call-done = f32[8,512]{1,0:T(8,128)} async-done(((f32[1024,512]{1,0:T(8,128)}), f32[8,512]{1,0:T(8,128)}) %reduce-scatter.4.cloned.1.call-update) | async-done | bytes 16400
  (119 shorter events, 47.7 us)
Async XLA Ops:
  8.1 6.5 collective-permute-start.1
  10.0 10.9 %collective-permute-start = (bf16[8,2,5120]{2,0,1:T(8,128)(2,1)S(1)}, bf16[8,2,5120]{2,0,1:T(8,128)(2,1)S(1)}, u32[]{:S(2)}, u32[]{:S(2)}) collective-permute-start(bf16[8,2,5120]{2,0,1:T(8,128)(2,1)S(1)} %copy.20), channel_id=1, source_target_pairs={{0,1},{1,2},{2,3},{4,5},{5,6},{6,7},{8,9},{9,10},{10,11},{12,13},{... | collective-permute-start | bytes 491528 | tf_op jit(solution)/shard_map/ppermute | solution.py:22
  29.2 4.7 collective-permute-start.3
  31.1 8.1 %collective-permute-start.2 = (bf16[8,2,5120]{2,0,1:T(8,128)(2,1)S(1)}, bf16[8,2,5120]{2,0,1:T(8,128)(2,1)S(1)}, u32[]{:S(2)}, u32[]{:S(2)}) collective-permute-start(bf16[8,2,5120]{2,0,1:T(8,128)(2,1)S(1)} %fusion.22), channel_id=1, source_target_pairs={{0,1},{1,2},{2,3},{4,5},{5,6},{6,7},{8,9},{9,10},{10,11},{12,13},{... | collective-permute-start | bytes 491528 | tf_op jit(solution)/shard_map/ppermute | solution.py:22
  44.4 2.3 copy-start
  47.9 4.7 collective-permute-start.5
  49.9 8.1 %collective-permute-start.4 = (bf16[8,2,5120]{2,0,1:T(8,128)(2,1)S(1)}, bf16[8,2,5120]{2,0,1:T(8,128)(2,1)S(1)}, u32[]{:S(2)}, u32[]{:S(2)}) collective-permute-start(bf16[8,2,5120]{2,0,1:T(8,128)(2,1)S(1)} %fusion.23), channel_id=1, source_target_pairs={{0,1},{1,2},{2,3},{4,5},{5,6},{6,7},{8,9},{9,10},{10,11},{12,13},{... | collective-permute-start | bytes 491528 | tf_op jit(solution)/shard_map/ppermute | solution.py:22
  66.6 4.7 collective-permute-start.7
  68.5 8.1 %collective-permute-start.6 = (bf16[8,2,5120]{2,0,1:T(8,128)(2,1)S(1)}, bf16[8,2,5120]{2,0,1:T(8,128)(2,1)S(1)}, u32[]{:S(2)}, u32[]{:S(2)}) collective-permute-start(bf16[8,2,5120]{2,0,1:T(8,128)(2,1)S(1)} %fusion.26), channel_id=1, source_target_pairs={{0,1},{1,2},{2,3},{4,5},{5,6},{6,7},{8,9},{9,10},{10,11},{12,13},{... | collective-permute-start | bytes 491528 | tf_op jit(solution)/shard_map/ppermute | solution.py:22
  85.3 24.9 %collective-permute-start.9 = (bf16[8,2,5120]{2,0,1:T(8,128)(2,1)S(1)}, bf16[8,2,5120]{2,0,1:T(8,128)(2,1)S(1)}, u32[]{:S(2)}, u32[]{:S(2)}) collective-permute-start(bf16[8,2,5120]{2,0,1:T(8,128)(2,1)S(1)} %fusion.29), channel_id=1, source_target_pairs={{1,0},{2,1},{3,2},{5,4},{6,5},{7,6},{9,8},{10,9},{11,10},{13,12},{... | collective-permute-start | bytes 491528 | tf_op jit(solution)/shard_map/ppermute | solution.py:24
  87.4 22.9 %collective-permute-start.8 = (bf16[8,2,5120]{2,0,1:T(8,128)(2,1)S(1)}, bf16[8,2,5120]{2,0,1:T(8,128)(2,1)S(1)}, u32[]{:S(2)}, u32[]{:S(2)}) collective-permute-start(bf16[8,2,5120]{2,0,1:T(8,128)(2,1)S(1)} %fusion.29), channel_id=1, source_target_pairs={{0,1},{1,2},{2,3},{4,5},{5,6},{6,7},{8,9},{9,10},{10,11},{12,13},{... | collective-permute-start | bytes 491528 | tf_op jit(solution)/shard_map/ppermute | solution.py:22
  91.0 38.1 %all-to-all-start = ((bf16[8,128,80]{2,0,1:T(8,128)(2,1)}), bf16[8,128,80]{2,0,1:T(8,128)(2,1)}, u32[]{:S(2)}, u32[]{:S(2)}) async-start(bf16[8,128,80]{2,0,1:T(8,128)(2,1)} %copy.26), calls=%async_computation | async-start | bytes 524288 | tf_op jit(solution)/shard_map/all_to_all | solution.py:87
  129.1 27.9 %all-to-all-start.1 = ((bf16[8,128,80]{2,0,1:T(8,128)(2,1)}), bf16[8,128,80]{2,0,1:T(8,128)(2,1)S(1)}, u32[]{:S(2)}, u32[]{:S(2)}) async-start(bf16[8,128,80]{2,0,1:T(8,128)(2,1)} %copy.29), calls=%async_computation.1 | async-start | bytes 524288 | tf_op jit(solution)/shard_map/all_to_all | solution.py:88
  138.2 650.0 %reduce-scatter.4.cloned.1.call-start = ((), (), s32[]{:S(2)}) async-start(), calls=%async_computation.3 | async-start | bytes 2113536
Sparse Core Ops, SparseCore 0:
  168.1 620.0 reduce-scatter.3
where the time goes:
time: 798 us; the launch traced here: 797 us
  waiting for transfers between devices  662 us (83%)
  starting transfers between devices  50.2 us (6%)
  local copies, waits for them, and re-layouts  33.8 us (4%)
  other arithmetic  17.8 us (2%)
  blocking collectives  17.4 us (2%)
  between operations  14.7 us (2%)
    unnamed x2, waiting for transfers between devices  620 us
    ppermute x5, waiting for transfers between devices, padded_2(): lax.ppermute(tail, axis, [(i, (i + 1) % count) for i in range(ends)])  22.1 us
    all_to_all x1, starting transfers between devices, per_device(): lax.all_to_all(filtered, 'band', split_axis=1, concat_axis=0, tiled=True)  19.2 us
  transfers between devices with their start and end apart: 13, of which 10 were waited for; matrix products, arithmetic and copies ran while one was open for 2% of the time, Pallas kernels for 0%

commit v1 on v0

--- a/solution.py
+++ b/solution.py
@@ -85,7 +85,12 @@
     applied = applied.reshape(orb_count, -1)
     cell_y, cell_h = (
         lax.all_to_all(filtered, "band", split_axis=1, concat_axis=0, tiled=True),
-        lax.all_to_all(applied, "band", split_axis=1, concat_axis=0, tiled=True),
+        jnp.concatenate(
+            lax.all_to_all(
+                jnp.stack(jnp.split(applied, lax.axis_size("band"), axis=1)), "band", 0, 0
+            ),
+            axis=0,
+        ),
     )
     cell_y, cell_h = (
         lax.all_gather(cell_y, "domain", axis=1, tiled=True),

time: 798 us -> 876 us (1.098)
  local copies, waits for them, and re-layouts: 33.8 us -> 115 us
  waiting for transfers between devices: 662 us -> 652 us
    unnamed x8 -> x135, local copies, waits for them, and re-layouts: 4.38 us -> 86.2 us
    all_to_all x1, waiting for transfers between devices: 11 us -> 0.01 us  [per_device(): lax.all_to_all(filtered, 'band', split_axis=1, concat_axis=0, tiled=True)]
  transfers between devices with their start and end apart: 13 -> 13, of which waited for: 10 -> 9; matrix products, arithmetic and copies ran while one was open for 2% -> 11% of each run, Pallas kernels for 0% -> 0%
where the time goes in v1:
time: 876 us; the launch traced here: 875 us
  waiting for transfers between devices  652 us (74%)
  local copies, waits for them, and re-layouts  115 us (13%)
  starting transfers between devices  58 us (7%)
  other arithmetic  17.8 us (2%)
  blocking collectives  17.3 us (2%)
  between operations  14.8 us (2%)
    unnamed x2, waiting for transfers between devices  620 us
    unnamed x135, local copies, waits for them, and re-layouts  86.2 us
    ppermute x5, waiting for transfers between devices, padded_2(): lax.ppermute(tail, axis, [(i, (i + 1) % count) for i in range(ends)])  22.1 us
    all_to_all x1, starting transfers between devices, per_device(): lax.all_to_all(filtered, 'band', split_axis=1, concat_axis=0, tiled=True)  19.2 us
  transfers between devices with their start and end apart: 13, of which 9 were waited for; matrix products, arithmetic and copies ran while one was open for 11% of the time, Pallas kernels for 0%

profile of v1, /device:TPU:4, one launch (start us, length us, event | category | flops | bytes accessed | tf_op | source)
XLA Modules:
  0.0 875.5 jit_solution(1252765614496343046)
XLA Ops:
  8.1 1.9 collective-permute-start.1
  10.0 2.4 collective-permute-start
  14.7 6.3 collective-permute-done
  29.2 1.9 collective-permute-start.3
  31.1 2.4 collective-permute-start.2
  34.0 5.3 collective-permute-done.2
  44.4 2.0 fusion.5
  47.9 1.9 collective-permute-start.5
  49.9 2.4 collective-permute-start.4
  52.7 5.3 collective-permute-done.4
  63.2 2.0 fusion.9
  66.6 1.9 collective-permute-start.7
  68.5 2.6 collective-permute-start.6
  71.4 5.3 collective-permute-done.6
  81.8 2.0 fusion.13
  85.3 1.9 collective-permute-start.9
  87.4 2.4 collective-permute-start.8
  91.0 19.2 %all-to-all-start = ((bf16[8,128,80]{2,0,1:T(8,128)(2,1)}), bf16[8,128,80]{2,0,1:T(8,128)(2,1)}, u32[]{:S(2)}, u32[]{:S(2)}) async-start(bf16[8,128,80]{2,0,1:T(8,128)(2,1)} %copy.24), calls=%async_computation | async-start | bytes 524288 | tf_op jit(solution)/shard_map/all_to_all | solution.py:87
  199.3 16.9 %all-to-all-start.1 = ((bf16[128,8,80]{2,1,0:T(8,128)(2,1)}), bf16[128,8,80]{2,1,0:T(8,128)(2,1)S(1)}, u32[]{:S(2)}, u32[]{:S(2)}) async-start(bf16[128,8,80]{2,1,0:T(8,128)(2,1)} %constant_dynamic-update-slice_fusion), calls=%async_computation.1 | async-start | bytes 524288 | tf_op jit(solution)/shard_map/all_to_all | solution.py:89
  217.3 8.9 %all_gather.6 = bf16[1024,320]{0,1:T(8,128)(2,1)S(1)} all-gather(bf16[1024,80]{0,1:T(8,128)(2,1)S(1)} %copy.25), channel_id=1, replica_groups=mesh['band'=128,'domain'=4] {'domain'}, dimensions={1}, use_global_device_ids=true | all-gather | bytes 819200 | tf_op jit(solution)/shard_map/all_gather | solution.py:96
  226.8 8.2 all-to-all-done.1
  235.1 8.4 all_gather.7
  244.2 1.8 copy.29
  246.0 620.2 %reduce-scatter.4.cloned.1.call-done = f32[8,512]{1,0:T(8,128)} async-done(((f32[1024,512]{1,0:T(8,128)}), f32[8,512]{1,0:T(8,128)}) %reduce-scatter.4.cloned.1.call-update) | async-done | bytes 16400
  (244 shorter events, 127.0 us)
Async XLA Ops:
  8.1 6.5 collective-permute-start.1
  10.0 10.9 %collective-permute-start = (bf16[8,2,5120]{2,0,1:T(8,128)(2,1)S(1)}, bf16[8,2,5120]{2,0,1:T(8,128)(2,1)S(1)}, u32[]{:S(2)}, u32[]{:S(2)}) collective-permute-start(bf16[8,2,5120]{2,0,1:T(8,128)(2,1)S(1)} %copy.18), channel_id=1, source_target_pairs={{0,1},{1,2},{2,3},{4,5},{5,6},{6,7},{8,9},{9,10},{10,11},{12,13},{... | collective-permute-start | bytes 491528 | tf_op jit(solution)/shard_map/ppermute | solution.py:22
  29.2 4.7 collective-permute-start.3
  31.1 8.1 collective-permute-start.2
  44.4 2.3 copy-start
  47.9 4.7 collective-permute-start.5
  49.9 8.1 collective-permute-start.4
  66.6 4.7 collective-permute-start.7
  68.5 8.1 collective-permute-start.6
  85.3 24.9 %collective-permute-start.9 = (bf16[8,2,5120]{2,0,1:T(8,128)(2,1)S(1)}, bf16[8,2,5120]{2,0,1:T(8,128)(2,1)S(1)}, u32[]{:S(2)}, u32[]{:S(2)}) collective-permute-start(bf16[8,2,5120]{2,0,1:T(8,128)(2,1)S(1)} %fusion.29), channel_id=1, source_target_pairs={{1,0},{2,1},{3,2},{5,4},{6,5},{7,6},{9,8},{10,9},{11,10},{13,12},{... | collective-permute-start | bytes 491528 | tf_op jit(solution)/shard_map/ppermute | solution.py:24
  87.4 22.9 %collective-permute-start.8 = (bf16[8,2,5120]{2,0,1:T(8,128)(2,1)S(1)}, bf16[8,2,5120]{2,0,1:T(8,128)(2,1)S(1)}, u32[]{:S(2)}, u32[]{:S(2)}) collective-permute-start(bf16[8,2,5120]{2,0,1:T(8,128)(2,1)S(1)} %fusion.29), channel_id=1, source_target_pairs={{0,1},{1,2},{2,3},{4,5},{5,6},{6,7},{8,9},{9,10},{10,11},{12,13},{... | collective-permute-start | bytes 491528 | tf_op jit(solution)/shard_map/ppermute | solution.py:22
  91.0 108.3 %all-to-all-start = ((bf16[8,128,80]{2,0,1:T(8,128)(2,1)}), bf16[8,128,80]{2,0,1:T(8,128)(2,1)}, u32[]{:S(2)}, u32[]{:S(2)}) async-start(bf16[8,128,80]{2,0,1:T(8,128)(2,1)} %copy.24), calls=%async_computation | async-start | bytes 524288 | tf_op jit(solution)/shard_map/all_to_all | solution.py:87
  199.3 35.7 %all-to-all-start.1 = ((bf16[128,8,80]{2,1,0:T(8,128)(2,1)}), bf16[128,8,80]{2,1,0:T(8,128)(2,1)S(1)}, u32[]{:S(2)}, u32[]{:S(2)}) async-start(bf16[128,8,80]{2,1,0:T(8,128)(2,1)} %constant_dynamic-update-slice_fusion), calls=%async_computation.1 | async-start | bytes 524288 | tf_op jit(solution)/shard_map/all_to_all | solution.py:89
  216.2 650.1 %reduce-scatter.4.cloned.1.call-start = ((), (), s32[]{:S(2)}) async-start(), calls=%async_computation.3 | async-start | bytes 2113536
Sparse Core Ops, SparseCore 0:
  246.2 620.0 reduce-scatter.3
